TPU v7x, 1024 devices: a whole 8x8x8 slice. The times are simulated.
1024 devices in a mesh: ka: 64 (over x_lo, y, core), ga: 16 (over z, x_hi).
Axes of the slice: x: 8 (x_hi: 2, x_lo: 4; x = x_hi * 4 + x_lo), y: 8, z: 8, core: 2. Of those that a mesh axis runs over, the one named last changes fastest.
Arguments:
- band_coefs: bfloat16 [64, 16, 2, 2048], P('ka'), may hold values from -12 to 12
- screening: bfloat16 [1, 2048, 2048], P(None, 'ga'), may hold values from -0.125 to 0.125
- grid_index: int32 [2048], replicated, may hold values from 1 to 4095, as said below
Outputs:
- kernel: float32 [64, 1, 64, 128], P('ka', None, 'ga')
Inputs may be any that keep to these rules, and one draw needn't show every extreme that they name: `grid_index`: the 2048 values are distinct flat grid indices x * 16 * 16 + y * 16 + z; the anchor 0 never appears.
All inputs are finite; a program needn't handle non-finite values.
Results may differ from a plain program's by a relative error of at most 0.0049.
Values may be sent and summed in bfloat16 or wider, within the bound.
No kernel may reach another device: no remote copies, remote signals or barrier semaphores. Data moves between devices by JAX's collectives and lax.ppermute only.
A program may use at most 32 MiB of HBM per device.

v0:
```python
import math

import jax
import jax.numpy as jnp
from jax import lax
from jax.sharding import PartitionSpec as P

NBND = 8
NG = 2048
NFFT = 16


def passed_along(value, axis, by):
    size = lax.axis_size(axis)
    return lax.ppermute(value, axis, [(i, (i + by) % size) for i in range(size)])


def make_table(phase, count, norm, sign):
    angle = phase.astype(jnp.float32) * (2.0 * math.pi / count)
    cosine = jnp.cos(angle) / norm
    sine = sign * jnp.sin(angle) / norm
    return jnp.stack([jnp.stack([cosine, sine]), jnp.stack([-sine, cosine])])


def line_table(count, sign):
    index = jnp.arange(count, dtype=jnp.int32)
    phase = index[:, None] * index[None, :] % count
    return make_table(phase, count, math.sqrt(count), sign)


def plane_table(count, sign):
    index = jnp.arange(count * count, dtype=jnp.int32)
    row_part = index // count
    col_part = index % count
    phase = (
        row_part[:, None] * row_part[None, :] % count
        + col_part[:, None] * col_part[None, :] % count
    ) % count
    return make_table(phase, count, float(count), sign)


def transform(field, tables):
    level = lax.Precision.HIGH
    field = jnp.einsum("bcxm,cdxu->bdum", field, tables[0], precision=level)
    return jnp.einsum("bcxm,cdmn->bdxn", field, tables[1], precision=level)


def to_grid(coeffs, grid_index):
    bands = coeffs.shape[0]
    waves = coeffs.shape[2]
    rows_flat = coeffs.reshape(bands * 2, waves)
    total = NFFT * NFFT * NFFT
    block = math.gcd(total, 512)
    count = total // block

    def one_block(first_point):
        points = first_point + jnp.arange(block, dtype=jnp.int32)
        selector = (grid_index[:, None] == points[None, :]).astype(jnp.bfloat16)
        return jnp.dot(rows_flat, selector, preferred_element_type=jnp.float32)

    starts = jnp.arange(count, dtype=jnp.int32) * block
    pieces = lax.map(one_block, starts)
    flat = jnp.transpose(pieces, (1, 0, 2)).reshape(bands, 2, total)
    return flat.reshape(bands, 2, NFFT, NFFT * NFFT)


def pair_density(first, second, grid_index, tables):
    real_part = first[:, None, 0] * second[None, :, 0] + first[:, None, 1] * second[None, :, 1]
    imag_part = first[:, None, 0] * second[None, :, 1] - first[:, None, 1] * second[None, :, 0]
    pairs = first.shape[0] * second.shape[0]
    field = jnp.stack([real_part, imag_part], axis=2).reshape(pairs, 2, NFFT, NFFT * NFFT)
    spectrum = transform(field, tables).reshape(pairs, 2, NFFT * NFFT * NFFT)
    return jnp.take(spectrum, grid_index, axis=2).astype(jnp.bfloat16)


def body(band_coefs, screening, grid_index):
    width = lax.axis_size("ga")
    place = lax.axis_index("ga")
    pair_count = NBND * NBND
    per_device = 2 * NBND // width
    start_own = place * per_device
    start_kind = start_own // NBND * NBND
    local = band_coefs[0]
    forward = (line_table(NFFT, -1.0), plane_table(NFFT, -1.0))
    inverse = (line_table(NFFT, 1.0), plane_table(NFFT, 1.0))
    own_bands = lax.dynamic_slice_in_dim(local, start_own, per_device, 0)
    first = transform(to_grid(own_bands, grid_index), inverse)
    moving = lax.dynamic_slice_in_dim(local, start_kind, NBND, 0)
    strip = screening.shape[1]
    scale = 1.0 / math.sqrt(NG)
    moving = passed_along(moving, "ka", 1)
    second = transform(to_grid(moving, grid_index), inverse)
    density = pair_density(first, second, grid_index, forward)
    weights = screening[0]
    strips = lax.all_to_all(density, "ga", split_axis=2, concat_axis=0, tiled=True)
    conduction = strips[pair_count:]
    piece = lax.all_gather(strips[:pair_count], "ga", axis=2, tiled=True)
    rows_flat = piece.reshape(piece.shape[0] * 2, piece.shape[2])
    mixed = lax.dot_general(
        rows_flat, weights, (((1,), (1,)), ((), ())), preferred_element_type=jnp.float32
    )
    screened = mixed.astype(jnp.bfloat16).reshape(pair_count, 2, strip)
    left = conduction.reshape(pair_count, 2 * strip)
    right_real = screened.reshape(pair_count, 2 * strip)
    right_imag = jnp.concatenate([screened[:, 1], -screened[:, 0]], axis=1)
    dims = (((1,), (1,)), ((), ()))
    real_block = lax.dot_general(left, right_real, dims, preferred_element_type=jnp.float32)
    imag_block = lax.dot_general(left, right_imag, dims, preferred_element_type=jnp.float32)
    terms = jnp.concatenate([real_block, imag_block], axis=1) * scale
    results = [lax.psum_scatter(terms, "ga", scatter_dimension=0, tiled=True)]
    return jnp.stack(results)[None]


def solution(mesh):
    return jax.shard_map(
        body,
        mesh=mesh,
        in_specs=(P("ka", None, None, None), P(None, "ga", None), P()),
        out_specs=P("ka", None, "ga", None),
        check_vma=False,
    )
```

profile of v0, /device:TPU:2, one launch (start us, length us, event | category | flops | bytes accessed | tf_op | source)
XLA Modules:
  0.0 268.1 jit_solution(13886275368118286554)
XLA Ops:
  0.0 0.9 dynamic-slice_bitcast_fusion
  0.9 1.9 collective-permute-start
  5.4 22.0 %while.20 = (s32[]{:T(128)}, f32[8,2,512]{2,1,0:T(2,128)S(1)}, s32[2048]{0:T(1024)}, s32[8]{0:T(128)S(1)}, bf16[2,2048]{1,0:T(2,128)(2,1)S(1)}, /*index=5*/s32[]{:T(128)}) while((s32[]{:T(128)}, f32[8,2,512]{2,1,0:T(2,128)S(1)}, s32[2048]{0:T(1024)}, s32[8]{0:T(128)S(1)}, bf16[2,2048]{1,0:T(2,128)(2,1)S(1)}, /*index=5*/s32[]{:T(128)}) %tuple.49), condition=%wide.region_1.2_spmd, body=%wide.region_0.1_spmd.sunk | while | flops 5243394 | bytes 24673 | solution.py:62
  6.6 1.5 fusion.88
  9.4 1.5 fusion.88
  12.1 1.5 fusion.88
  14.9 1.5 fusion.88
  17.6 1.5 fusion.88
  20.4 1.5 fusion.88
  23.1 1.5 fusion.88
  25.9 1.5 fusion.88
  27.4 1.3 broadcast_multiply_fusion
  29.7 16.4 %while.21 = (s32[]{:T(128)}, f32[8,16,512]{2,1,0:T(8,128)S(1)}, s32[2048]{0:T(1024)S(1)}, s32[8]{0:T(128)S(1)}, bf16[16,2048]{1,0:T(8,128)(2,1)S(1)}, /*index=5*/s32[]{:T(128)}) while((s32[]{:T(128)}, f32[8,16,512]{2,1,0:T(8,128)S(1)}, s32[2048]{0:T(1024)S(1)}, s32[8]{0:T(128)S(1)}, bf16[16,2048]{1,0:T(8,128)(2,1)S(1)}, ...), condition=%wide.region_3.4_spmd, body=%wide.region_2.3_spmd.sunk | while | flops 34603520 | bytes 110689 | solution.py:62
  30.9 0.8 fusion.91
  47.9 1.2 copy.55
  49.1 13.8 %gather_fusion = bf16[2048,8,2]{1,2,0:T(2,128)(2,1)} fusion(bf16[8,2,4096]{0,1,2:T(2,128)(2,1)S(1)} %bitcast.160, s32[2048]{0:T(1024)S(1)} %fusion.61), kind=kCustom, calls=%fused_computation | custom fusion | bytes 139264 | tf_op jit(solution)/shard_map/jit(_take)/gather | solution.py:73
  63.0 9.8 %fusion.71 = bf16[2048,2,8]{2,1,0:T(2,128)(2,1)S(1)} fusion(bf16[2048,8,2]{1,2,0:T(2,128)(2,1)} %gather_fusion, pred[2048]{0:T(1024)(128)(4,1)S(1)} %compare_and_fusion), kind=kLoop, calls=%fused_computation.130 | loop fusion | flops 32768 | bytes 133120
  72.7 1.7 reshape.835
  74.4 20.8 %all-to-all-start = ((bf16[16,2,1024]{2,1,0:T(2,128)(2,1)}), bf16[16,2,1024]{2,1,0:T(2,128)(2,1)S(1)}, u32[]{:S(2)}, u32[]{:S(2)}) async-start(bf16[16,2,1024]{2,1,0:T(2,128)(2,1)} %reshape.835), calls=%async_computation | async-start | bytes 131072 | tf_op jit(solution)/shard_map/all_to_all | solution.py:95
  95.3 1.3 dynamic-slice.2
  97.2 11.0 %all-to-all-done = bf16[16,2,1024]{2,1,0:T(2,128)(2,1)S(1)} async-done(((bf16[16,2,1024]{2,1,0:T(2,128)(2,1)}), bf16[16,2,1024]{2,1,0:T(2,128)(2,1)S(1)}, u32[]{:S(2)}, u32[]{:S(2)}) %all-to-all-start) | async-done | bytes 65568 | tf_op jit(solution)/shard_map/all_to_all | solution.py:95
  108.2 1.2 reshape.836
  110.0 58.2 %all_gather.3 = bf16[64,2,2048]{2,0,1:T(8,128)(2,1)S(1)} all-gather(bf16[64,2,128]{2,0,1:T(8,128)(2,1)S(1)} %copy_bitcast_fusion), channel_id=1, replica_groups=mesh['ka'=64,'ga'=16] {'ga'}, dimensions={2}, use_global_device_ids=true | all-gather | bytes 557056 | tf_op jit(solution)/shard_map/all_gather | solution.py:97
  169.6 97.9 %all-reduce = f32[64,128]{1,0:T(8,128)S(1)} all-reduce(f32[64,128]{1,0:T(8,128)S(1)} %maximum_multiply_fusion), channel_id=2, replica_groups=mesh['ka'=64,'ga'=16] {'ga'}, use_global_device_ids=true, to_apply=%region_4.5.clone | all-reduce | flops 8192 | bytes 65536
  (85 shorter events, 33.2 us)
Async XLA Ops:
  0.0 168.9 %copy-start = (bf16[1,128,2048]{2,1,0:T(8,128)(2,1)S(1)}, bf16[1,128,2048]{2,1,0:T(8,128)(2,1)}, u32[]{:S(2)}) copy-start(bf16[1,128,2048]{2,1,0:T(8,128)(2,1)} %param.8) | copy-start | bytes 1572868
  0.9 28.6 %collective-permute-start = (bf16[8,2,2048]{2,1,0:T(2,128)(2,1)S(1)}, bf16[8,2,2048]{2,1,0:T(2,128)(2,1)S(1)}, u32[]{:S(2)}, u32[]{:S(2)}) collective-permute-start(bf16[8,2,2048]{2,1,0:T(2,128)(2,1)S(1)} %dynamic-slice_bitcast_fusion), channel_id=1, source_target_pairs={{0,16},{16,32},{32,48},{48,64},{64,80},{80,96},{96,112},{112,128},... | collective-permute-start | bytes 196616 | tf_op jit(solution)/shard_map/ppermute | solution.py:15
  29.0 0.7 copy-start.1
  74.4 33.8 %all-to-all-start = ((bf16[16,2,1024]{2,1,0:T(2,128)(2,1)}), bf16[16,2,1024]{2,1,0:T(2,128)(2,1)S(1)}, u32[]{:S(2)}, u32[]{:S(2)}) async-start(bf16[16,2,1024]{2,1,0:T(2,128)(2,1)} %reshape.835), calls=%async_computation | async-start | bytes 131072 | tf_op jit(solution)/shard_map/all_to_all | solution.py:95
where the time goes:
time: 269 us; the launch traced here: 268 us
  blocking collectives  156 us (58%)
  local copies, waits for them, and re-layouts  32.9 us (12%)
  other arithmetic  23.3 us (9%)
  starting transfers between devices  22.7 us (8%)
  matrix products  21 us (8%)
  waiting for transfers between devices  11 us (4%)
    unnamed x1, blocking collectives  97.9 us
    all_gather x1, blocking collectives, body(): piece = lax.all_gather(strips[:pair_count], 'ga', axis=2, tiled=True)  58.2 us
    all_to_all x1, starting transfers between devices, body(): lax.all_to_all(density, 'ga', split_axis=2, concat_axis=0, tiled=True)  20.8 us
    dot_general x16, matrix products, one_block(): return jnp.dot(rows_flat, selector, preferred_element_type=jnp.float32)  18.4 us
    gather x1, local copies, waits for them, and re-layouts, pair_density(): return jnp.take(spectrum, grid_index, axis=2).astype(jnp.bfloat16)  13.8 us
    all_to_all x1, waiting for transfers between devices, body(): lax.all_to_all(density, 'ga', split_axis=2, concat_axis=0, tiled=True)  11 us
    add x16, other arithmetic, one_block(): points = first_point + jnp.arange(block, dtype=jnp.int32)  10.2 us
    dynamic_slice x16, local copies, waits for them, and re-layouts, to_grid(): pieces = lax.map(one_block, starts)  9.78 us
  transfers between devices with their start and end apart: 2, of which 1 were waited for; matrix products, arithmetic and copies ran while one was open for 10% of the time, Pallas kernels for 0%

commit v1 on v0

v1 whole, which is shorter than its diff:
```python
import math

import jax
import jax.numpy as jnp
import numpy as np
from jax import lax
from jax.experimental import pallas as pl
from jax.experimental.pallas import tpu as pltpu
from jax.sharding import PartitionSpec as P

NBND = 8
NG = 2048
NFFT = 16
PLANE = NFFT * NFFT
GRID = NFFT * PLANE
PAIRS = NBND * NBND
STEP = 1.130485
LEVEL = 1.1328025

NT = (((1,), (1,)), ((), ()))
NN = (((1,), (0,)), ((), ()))


def mm(left, right, dims=NN, precision=None):
    return lax.dot_general(left, right, dims, precision=precision, preferred_element_type=jnp.float32)


def plane_table():
    index = np.arange(PLANE)
    phase = np.outer(index // NFFT, index // NFFT) + np.outer(index % NFFT, index % NFFT)
    angle = (phase % NFFT) * (2.0 * math.pi / NFFT)
    return np.stack([np.cos(angle), np.sin(angle)]) * STEP


def radix4(a, b, c, d, sign):
    sr, si = a[0] + c[0], a[1] + c[1]
    dr, di = a[0] - c[0], a[1] - c[1]
    tr, ti = b[0] + d[0], b[1] + d[1]
    er, ei = b[0] - d[0], b[1] - d[1]
    plus = (dr - ei, di + er)
    minus = (dr + ei, di - er)
    first, third = (plus, minus) if sign > 0 else (minus, plus)
    return [(sr + tr, si + ti), first, (sr - tr, si - ti), third]


def turned(value, power, sign):
    if power == 0:
        return value
    re, im = value
    if power == 4:
        return (-im, re) if sign > 0 else (im, -re)
    c = math.cos(2.0 * math.pi * power / NFFT)
    s = sign * math.sin(2.0 * math.pi * power / NFFT)
    if power == 2:
        return ((re - im) * c, (re + im) * c) if sign > 0 else ((re + im) * c, (im - re) * c)
    if power == 6:
        return ((re + im) * c, (im - re) * c) if sign > 0 else ((re - im) * c, (re + im) * c)
    return (re * c - im * s, re * s + im * c)


def sixteen(values, sign):
    inner = [radix4(values[x], values[x + 4], values[x + 8], values[x + 12], sign) for x in range(4)]
    out = [None] * NFFT
    for u in range(4):
        group = radix4(*[turned(inner[x][u], x * u, sign) for x in range(4)], sign)
        for v in range(4):
            out[u + 4 * v] = group[v]
    return out


def selectors(index_ref, plane_ref, masks_ref):
    index = index_ref[...]
    rows = lax.broadcasted_iota(jnp.int32, (PLANE, NG), 0)
    plane_ref[...] = jnp.where(rows == (index & (PLANE - 1)), 1.0, 0.0).astype(jnp.bfloat16)
    levels = lax.broadcasted_iota(jnp.int32, (NFFT, NG), 0)
    masks_ref[...] = jnp.where(levels == (index >> 8), 1.0, 0.0).astype(jnp.bfloat16)


def orbital_kernel(index_ref, coefs_ref, table_ref, psi_ref, plane_ref, masks_ref, spread_ref, field_ref):
    selectors(index_ref, plane_ref, masks_ref)
    bands = 2 * NBND
    half = NFFT * bands
    for part in range(2):
        held = coefs_ref[part]
        for x in range(NFFT):
            spread_ref[pl.ds(part * half + x * bands, bands), :] = held * masks_ref[pl.ds(x, 1), :]
    planes = mm(spread_ref[...], plane_ref[...], NT).astype(jnp.bfloat16)
    field_ref[0] = mm(planes, table_ref[0])
    field_ref[1] = mm(planes, table_ref[1])
    for lane in range(0, PLANE, 128):
        at = pl.ds(lane, 128)
        values = []
        for x in range(NFFT):
            top, low = pl.ds(x * bands, bands), pl.ds(half + x * bands, bands)
            re = field_ref[0, top, at] - field_ref[1, low, at]
            im = field_ref[1, top, at] + field_ref[0, low, at]
            values.append((re, im))
        for u, (re, im) in enumerate(sixteen(values, 1)):
            psi_ref[0, :, pl.ds(u * PLANE + lane, 128)] = re
            psi_ref[1, :, pl.ds(u * PLANE + lane, 128)] = im


def screen_kernel(place_ref, index_ref, own_ref, weights_ref, table_ref, wide_ref, waves_ref,
                  plane_ref, masks_ref, spread_ref, field_ref):
    selectors(index_ref, plane_ref, masks_ref)
    strip = weights_ref.shape[0]
    group = 4

    def some_planes(step, carry):
        for x in range(group):
            mask = masks_ref[pl.ds(step * group + x, 1), :]
            spread_ref[pl.ds(x * strip, strip), :] = weights_ref[...] * mask
        planes = mm(spread_ref[...], plane_ref[...], NT).astype(jnp.bfloat16)
        rows = pl.ds(pl.multiple_of(step * (group * strip), group * strip), group * strip)
        field_ref[0, rows, :] = mm(planes, table_ref[0])
        field_ref[1, rows, :] = mm(planes, table_ref[1])
        return carry

    for step in range(NFFT // group):
        some_planes(step, 0)

    def some_rows(step, carry):
        first = pl.multiple_of(step * 16, 16)
        for lane in range(0, PLANE, 128):
            at = pl.ds(lane, 128)
            values = []
            for x in range(NFFT):
                rows = pl.ds(pl.multiple_of(x * strip + first, 16), 16)
                values.append((field_ref[0, rows, at], -field_ref[1, rows, at]))
            for u, (re, im) in enumerate(sixteen(values, -1)):
                out = pl.ds(u * PLANE + lane, 128)
                wide_ref[pl.ds(first, 16), out] = re.astype(jnp.bfloat16)
                wide_ref[pl.ds(pl.multiple_of(first + strip, 16), 16), out] = im.astype(jnp.bfloat16)
        return carry

    lax.fori_loop(0, strip // 16, some_rows, 0)

    chosen = plane_ref[:, pl.ds(pl.multiple_of(place_ref[0] * strip, strip), strip)]
    cos_plane = mm(table_ref[0], chosen)
    sin_plane = mm(table_ref[1], chosen)
    level = own_ref[...] >> 8
    turn = (level * lax.broadcasted_iota(jnp.int32, (NFFT, strip), 0)) & (NFFT - 1)
    angle = turn.astype(jnp.float32) * (2.0 * math.pi / NFFT)
    cos_line = jnp.cos(angle)
    sin_line = jnp.sin(angle)
    for u in range(NFFT):
        c, s = cos_line[u : u + 1, :], sin_line[u : u + 1, :]
        rows = pl.ds(u * PLANE, PLANE)
        waves_ref[rows, pl.ds(0, strip)] = (cos_plane * c - sin_plane * s).astype(jnp.bfloat16)
        waves_ref[rows, pl.ds(strip, strip)] = (-(sin_plane * c + cos_plane * s)).astype(jnp.bfloat16)


def contract_kernel(scale, here_ref, there_ref, wide_ref, waves_ref, out_ref, valence_ref, conduction_ref):
    strip = wide_ref.shape[0] // 2
    chunk = 512
    for lane in range(0, GRID, chunk):
        at = pl.ds(lane, chunk)
        for first, target in ((0, valence_ref), (NBND, conduction_ref)):
            br = there_ref[0, pl.ds(first, NBND), at]
            bi = there_ref[1, pl.ds(first, NBND), at]
            for v in range(0, NBND, 2):
                re, im = [], []
                for band in (first + v, first + v + 1):
                    ar = here_ref[0, pl.ds(band, 1), at]
                    ai = here_ref[1, pl.ds(band, 1), at]
                    re.append(ar * br + ai * bi)
                    im.append(ar * bi - ai * br)
                target[pl.ds(v * NBND, 2 * NBND), at] = jnp.concatenate(re, 0).astype(jnp.bfloat16)
                target[pl.ds(PAIRS + v * NBND, 2 * NBND), at] = jnp.concatenate(im, 0).astype(jnp.bfloat16)

    def joined(block):
        re = block[:PAIRS, :strip] - block[PAIRS:, strip:]
        im = block[:PAIRS, strip:] + block[PAIRS:, :strip]
        return re, im

    sr, si = joined(mm(valence_ref[...], wide_ref[...], NT))
    cr, ci = joined(mm(conduction_ref[...], waves_ref[...]))
    left = jnp.concatenate([cr, ci], 1)
    right = jnp.concatenate([jnp.concatenate([sr, si], 1), jnp.concatenate([si, -sr], 1)], 0)
    out_ref[...] = mm(left, right, NT, lax.Precision.HIGHEST) * scale


def passed_along(value, axis, by):
    size = lax.axis_size(axis)
    return lax.ppermute(value, axis, [(i, (i + by) % size) for i in range(size)])


def called(kernel, shapes, scratch, flops, moved, *args, smem=0):
    specs = [pl.BlockSpec(memory_space=pltpu.SMEM)] * smem
    specs += [pl.BlockSpec(memory_space=pltpu.VMEM)] * (len(args) - smem)
    out_specs = [pl.BlockSpec(memory_space=pltpu.VMEM) for _ in shapes]
    return pl.pallas_call(
        kernel,
        out_shape=shapes,
        in_specs=specs,
        out_specs=out_specs,
        scratch_shapes=scratch,
        cost_estimate=pl.CostEstimate(flops=flops, bytes_accessed=moved, transcendentals=0),
        compiler_params=pltpu.CompilerParams(vmem_limit_bytes=36 * 1024 * 1024),
    )(*args)


def orbitals(index, coefs, table):
    bands = coefs.shape[1]
    shape = jax.ShapeDtypeStruct((2, bands, GRID), jnp.float32)
    scratch = [
        pltpu.VMEM((PLANE, NG), jnp.bfloat16),
        pltpu.VMEM((NFFT, NG), jnp.bfloat16),
        pltpu.VMEM((2 * NFFT * bands, NG), jnp.bfloat16),
        pltpu.VMEM((2, 2 * NFFT * bands, PLANE), jnp.float32),
    ]
    return called(orbital_kernel, [shape], scratch, 10**9, 2**20, index, coefs, table)[0]


def screening_waves(place, index, own, weights, table):
    strip = weights.shape[0]
    shapes = [
        jax.ShapeDtypeStruct((2 * strip, GRID), jnp.bfloat16),
        jax.ShapeDtypeStruct((GRID, 2 * strip), jnp.bfloat16),
    ]
    scratch = [
        pltpu.VMEM((PLANE, NG), jnp.bfloat16),
        pltpu.VMEM((NFFT, NG), jnp.bfloat16),
        pltpu.VMEM((4 * strip, NG), jnp.bfloat16),
        pltpu.VMEM((2, NFFT * strip, PLANE), jnp.float32),
    ]
    return called(screen_kernel, shapes, scratch, 5 * 10**9, 2**23, place, index, own, weights, table, smem=1)


def contracted(here, there, wide, waves, scale):
    shape = jax.ShapeDtypeStruct((PAIRS, 2 * PAIRS), jnp.float32)
    scratch = [pltpu.VMEM((2 * PAIRS, GRID), jnp.bfloat16) for _ in range(2)]

    def kernel(*refs):
        contract_kernel(scale, *refs)

    return called(kernel, [shape], scratch, 10**9, 2**22, here, there, wide, waves)[0]


def body(band_coefs, screening, grid_index):
    width = lax.axis_size("ga")
    place = lax.axis_index("ga").astype(jnp.int32)
    strip = screening.shape[1]
    table = jnp.asarray(plane_table(), jnp.bfloat16)
    index = grid_index.reshape(1, NG)
    coefs = jnp.transpose(band_coefs[0], (1, 0, 2))
    here = orbitals(index, coefs, table)
    there = passed_along(here, "ka", 1)
    own = lax.dynamic_slice_in_dim(index, place * strip, strip, 1)
    wide, waves = screening_waves(place.reshape(1), index, own, screening[0], table)
    scale = 1.0 / (math.sqrt(NG) * (math.sqrt(GRID) * LEVEL) ** 6)
    terms = contracted(here, there, wide, waves, scale)
    rows = terms.shape[0] // width
    pieces = lax.all_to_all(terms.reshape(width, rows, 2 * PAIRS), "ga", 0, 0, tiled=True)
    return jnp.sum(pieces, axis=0)[None, None]


def solution(mesh):
    return jax.shard_map(
        body,
        mesh=mesh,
        in_specs=(P("ka", None, None, None), P(None, "ga", None), P()),
        out_specs=P("ka", None, "ga", None),
        check_vma=False,
    )
```

time: 269 us -> 52.7 us (0.20)
  blocking collectives: 156 us -> 33.9 us
  local copies, waits for them, and re-layouts: 32.9 us -> 2.73 us
  other arithmetic: 23.3 us -> 0.6 us
  matrix products: 21 us -> 0 us
  starting transfers between devices: 22.7 us -> 1.92 us
  Pallas kernels: 0 us -> 10 us
  waiting for transfers between devices: 11 us -> 3.21 us
    unnamed x1 -> x0, blocking collectives: 97.9 us -> none
    all_gather x1 -> x0, blocking collectives: 58.2 us -> none  [body(): piece = lax.all_gather(strips[:pair_count], 'ga', axis=2, tiled=True)]
    all_to_all x0 -> x1, blocking collectives: none -> 33.9 us  [body(): lax.all_to_all(terms.reshape(width, rows, 2 * PAIRS), 'ga', 0, 0, tiled=T...]
    dot_general x25 -> x0, matrix products: 21 us -> none  [the longest x16 18.4 us: one_block(): return jnp.dot(rows_flat, selector, preferred_element_type=jnp.float32)]
    all_to_all x1 -> x0, starting transfers between devices: 20.8 us -> none  [body(): lax.all_to_all(density, 'ga', split_axis=2, concat_axis=0, tiled=True)]
    gather x1 -> x0, local copies, waits for them, and re-layouts: 13.8 us -> none  [pair_density(): return jnp.take(spectrum, grid_index, axis=2).astype(jnp.bfloat16)]
    all_to_all x1 -> x0, waiting for transfers between devices: 11 us -> none  [body(): lax.all_to_all(density, 'ga', split_axis=2, concat_axis=0, tiled=True)]
    dynamic_slice x17 -> x1, local copies, waits for them, and re-layouts: 10.7 us -> 0.08 us  [body(): own = lax.dynamic_slice_in_dim(index, place * strip, strip, 1)]
  transfers between devices with their start and end apart: 2 -> 1, of which waited for: 1 -> 1; matrix products, arithmetic and copies ran while one was open for 10% -> 0% of each run, Pallas kernels for 0% -> 14%
where the time goes in v1:
time: 52.7 us; the launch traced here: 52.4 us
  blocking collectives  33.9 us (64%)
  Pallas kernels  10 us (19%)
  waiting for transfers between devices  3.21 us (6%)
  local copies, waits for them, and re-layouts  2.73 us (5%)
  starting transfers between devices  1.92 us (4%)
  other arithmetic  0.6 us (1%)
    all_to_all x1, blocking collectives, body(): lax.all_to_all(terms.reshape(width, rows, 2 * PAIRS), 'ga', 0, 0, tiled=T...  33.9 us
    pallas_call x3, Pallas kernels, called(): pl.pallas_call(kernel, out_shape=shapes, in_specs=specs, out_specs=out_sp...  10 us
    ppermute x1, waiting for transfers between devices, passed_along(): lax.ppermute(value, axis, [(i, (i + by) % size) for i in range(size)])  3.21 us
    unnamed x11, local copies, waits for them, and re-layouts  2.66 us
    ppermute x1, starting transfers between devices, passed_along(): lax.ppermute(value, axis, [(i, (i + by) % size) for i in range(size)])  1.92 us
  transfers between devices with their start and end apart: 1, of which 1 were waited for; matrix products, arithmetic and copies ran while one was open for 0% of the time, Pallas kernels for 14%

profile of v1, /device:TPU:2, one launch (start us, length us, event | category | flops | bytes accessed | tf_op | source)
XLA Modules:
  0.0 52.4 jit_solution(7152244183042971800)
XLA Ops:
  0.0 0.0 copy-start
  0.0 1.0 %copy.7 = bf16[1,16,2,2048]{3,1,2,0:T(8,128)(2,1)S(1)} copy(bf16[1,16,2,2048]{3,2,1,0:T(2,128)(2,1)} %param.4) | data formatting | bytes 262144 | tf_op args[0]
  1.0 0.0 copy-start.1
  1.0 0.7 %copy-done.1 = s32[2048]{0:T(1024)S(1)} copy-done((s32[2048]{0:T(1024)S(1)}, s32[2048]{0:T(1024)}, u32[]{:S(2)}) %copy-start.1) | copy-done | bytes 8216
  1.7 0.0 copy-start.3
  1.7 0.9 %copy-done.3 = bf16[2,256,256]{2,1,0:T(8,128)(2,1)S(1)} copy-done((bf16[2,256,256]{2,1,0:T(8,128)(2,1)S(1)}, bf16[2,256,256]{2,1,0:T(8,128)(2,1)}, u32[]{:S(2)}) %copy-start.3) | copy-done | bytes 262168
  2.7 0.0 copy-start.2
  2.7 0.0 copy-start.4
  2.7 1.2 %shard_map.46.refs_0_ = f32[2,16,4096]{2,1,0:T(8,128)S(1)} custom-call(s32[1,2048]{1,0:T(1,128)S(1)} %bitcast.15, bf16[2,16,2048]{2,1,0:T(8,128)(2,1)S(1)} %bitcast.13, bf16[2,256,256]{2,1,0:T(8,128)(2,1)S(1)} %copy-done.3), custom_call_target="tpu_custom_call" | custom-call | flops 1000000000 | bytes 1048576 | tf_op jit(solution)/shard_map/pallas_call | solution.py:192
  3.9 1.9 %collective-permute-start = (f32[2,16,4096]{2,1,0:T(8,128)S(1)}, f32[2,16,4096]{2,1,0:T(8,128)S(1)}, u32[]{:S(2)}, u32[]{:S(2)}) collective-permute-start(f32[2,16,4096]{2,1,0:T(8,128)S(1)} %shard_map.46.refs_0_), channel_id=1, source_target_pairs={{0,16},{16,32},{32,48},{48,64},{64,80},{80,96},{96,112},{112,128},... | collective-permute-start | bytes 1572872 | tf_op jit(solution)/shard_map/ppermute | solution.py:185
  5.8 0.0 copy-done.2
  5.8 0.1 dynamic-slice_bitcast_fusion.own_ref
  5.9 0.0 copy-done
  5.9 0.0 copy-done.4
  5.9 7.4 %shard_map.47 = (bf16[256,4096]{1,0:T(8,128)(2,1)S(1)}, bf16[4096,256]{1,0:T(8,128)(2,1)S(1)}) custom-call(s32[1]{0:T(128)} %bitcast.3.place_ref, s32[1,2048]{1,0:T(1,128)S(1)} %bitcast.16, s32[1,128]{1,0:T(1,128)S(1)} %dynamic-slice_bitcast_fusion.own_ref, bf16[128,2048]{1,0:T(8,128)(2,1)S(1)} %bitcast.14, bf16[2,256,256]{2,1,0:T(8,128)(2,1)S(1)} %copy-done.4), custom_call_target="tpu_custom_call" | custom-call | flops 5000000000 | bytes 8388608 | tf_op jit(solution)/shard_map/pallas_call | solution.py:192
  13.3 3.2 %collective-permute-done.refs_1_ = f32[2,16,4096]{2,1,0:T(8,128)S(1)} collective-permute-done((f32[2,16,4096]{2,1,0:T(8,128)S(1)}, f32[2,16,4096]{2,1,0:T(8,128)S(1)}, u32[]{:S(2)}, u32[]{:S(2)}) %collective-permute-start) | collective-permute-done | bytes 524320 | tf_op jit(solution)/shard_map/ppermute | solution.py:185
  16.5 1.4 %shard_map.48 = f32[64,128]{1,0:T(8,128)S(1)} custom-call(f32[2,16,4096]{2,1,0:T(8,128)S(1)} %shard_map.46.refs_0_, f32[2,16,4096]{2,1,0:T(8,128)S(1)} %collective-permute-done.refs_1_, bf16[256,4096]{1,0:T(8,128)(2,1)S(1)} %get-tuple-element.7.refs_2_, bf16[4096,256]{1,0:T(8,128)(2,1)S(1)} %get-tuple-element.8.refs_3_), custom_call_target="tpu_custom_call" | custom-call | flops 1000000000 | bytes 4194304 | tf_op jit(solution)/shard_map/pallas_call | solution.py:192
  17.9 33.9 %all_to_all.5 = f32[16,4,128]{2,1,0:T(4,128)S(1)} all-to-all(f32[16,4,128]{2,1,0:T(4,128)S(1)} %bitcast.12), channel_id=1, replica_groups=mesh['ka'=64,'ga'=16] {'ga'}, dimensions={0} | all-to-all | bytes 65536 | tf_op jit(solution)/shard_map/all_to_all | solution.py:254
  51.8 0.6 %reduce_sum.9 = f32[4,128]{1,0:T(4,128)} reduce(f32[16,4,128]{2,1,0:T(4,128)S(1)} %all_to_all.5, f32[]{:T(128)} %constant.5.clone.1), dimensions={0}, to_apply=%region_0.0 | reduce | flops 7680 | bytes 34820 | tf_op jit(solution)/shard_map/reduce_sum | solution.py:255
Async XLA Ops:
  0.0 5.9 %copy-start = (bf16[1,128,2048]{2,1,0:T(8,128)(2,1)S(1)}, bf16[1,128,2048]{2,1,0:T(8,128)(2,1)}, u32[]{:S(2)}) copy-start(bf16[1,128,2048]{2,1,0:T(8,128)(2,1)} %param.5) | copy-start | bytes 1572868
  1.0 0.7 %copy-start.1 = (s32[2048]{0:T(1024)S(1)}, s32[2048]{0:T(1024)}, u32[]{:S(2)}) copy-start(s32[2048]{0:T(1024)} %param.6) | copy-start | bytes 24580
  1.7 0.9 %copy-start.3 = (bf16[2,256,256]{2,1,0:T(8,128)(2,1)S(1)}, bf16[2,256,256]{2,1,0:T(8,128)(2,1)}, u32[]{:S(2)}) copy-start(bf16[2,256,256]{2,1,0:T(8,128)(2,1)} %constant.14.clone.table_ref) | copy-start | bytes 786436
  2.7 3.2 %copy-start.2 = (s32[2048]{0:T(1024)S(1)}, s32[2048]{0:T(1024)}, u32[]{:S(2)}) copy-start(s32[2048]{0:T(1024)} %param.6) | copy-start | bytes 24580
  2.7 3.3 %copy-start.4 = (bf16[2,256,256]{2,1,0:T(8,128)(2,1)S(1)}, bf16[2,256,256]{2,1,0:T(8,128)(2,1)}, u32[]{:S(2)}) copy-start(bf16[2,256,256]{2,1,0:T(8,128)(2,1)} %constant.14.clone.table_ref) | copy-start | bytes 786436
  3.9 12.6 %collective-permute-start = (f32[2,16,4096]{2,1,0:T(8,128)S(1)}, f32[2,16,4096]{2,1,0:T(8,128)S(1)}, u32[]{:S(2)}, u32[]{:S(2)}) collective-permute-start(f32[2,16,4096]{2,1,0:T(8,128)S(1)} %shard_map.46.refs_0_), channel_id=1, source_target_pairs={{0,16},{16,32},{32,48},{48,64},{64,80},{80,96},{96,112},{112,128},... | collective-permute-start | bytes 1572872 | tf_op jit(solution)/shard_map/ppermute | solution.py:185

commit v2 on v1

--- a/solution.py
+++ b/solution.py
@@ -76,15 +76,16 @@
     masks_ref[...] = jnp.where(levels == (index >> 8), 1.0, 0.0).astype(jnp.bfloat16)
 
 
-def orbital_kernel(index_ref, coefs_ref, table_ref, psi_ref, plane_ref, masks_ref, spread_ref, field_ref):
-    selectors(index_ref, plane_ref, masks_ref)
+def fill_orbitals(coefs_ref, table_ref, plane_ref, masks_ref, psi_ref, spread_ref, field_ref, copy=None):
     bands = 2 * NBND
     half = NFFT * bands
     for part in range(2):
-        held = coefs_ref[part]
+        held = coefs_ref[:, part, :]
         for x in range(NFFT):
             spread_ref[pl.ds(part * half + x * bands, bands), :] = held * masks_ref[pl.ds(x, 1), :]
     planes = mm(spread_ref[...], plane_ref[...], NT).astype(jnp.bfloat16)
+    if copy is not None:
+        copy.wait()
     field_ref[0] = mm(planes, table_ref[0])
     field_ref[1] = mm(planes, table_ref[1])
     for lane in range(0, PLANE, 128):
@@ -100,24 +101,43 @@
             psi_ref[1, :, pl.ds(u * PLANE + lane, 128)] = im
 
 
-def screen_kernel(place_ref, index_ref, own_ref, weights_ref, table_ref, wide_ref, waves_ref,
-                  plane_ref, masks_ref, spread_ref, field_ref):
+def prepare_kernel(place_ref, index_hbm, coefs_hbm, weights_hbm, table_hbm,
+                   psi_ref, wide_ref, waves_ref, plane_ref, masks_ref,
+                   small_ref, small_field_ref, spread_ref, planes_ref, field_ref,
+                   index_ref, coefs_ref, weights_ref, table_ref, sems):
+    pairs = ((index_hbm, index_ref), (weights_hbm, weights_ref), (table_hbm, table_ref), (coefs_hbm, coefs_ref))
+    copies = [pltpu.make_async_copy(source, target, sems.at[i]) for i, (source, target) in enumerate(pairs)]
+    for copy in copies:
+        copy.start()
+    copies[0].wait()
     selectors(index_ref, plane_ref, masks_ref)
     strip = weights_ref.shape[0]
+    first_own = pl.multiple_of(place_ref[0] * strip, strip)
+    level = index_ref[:, pl.ds(first_own, strip)] >> 8
+    turn = (level * lax.broadcasted_iota(jnp.int32, (NFFT, strip), 0)) & (NFFT - 1)
+    angle = turn.astype(jnp.float32) * (2.0 * math.pi / NFFT)
+    cos_line = jnp.cos(angle)
+    sin_line = jnp.sin(angle)
+    copies[1].wait()
+    copies[2].wait()
+    chosen = plane_ref[:, pl.ds(first_own, strip)]
+    cos_plane = mm(table_ref[0], chosen)
+    sin_plane = mm(table_ref[1], chosen)
     group = 4
-
-    def some_planes(step, carry):
-        for x in range(group):
-            mask = masks_ref[pl.ds(step * group + x, 1), :]
-            spread_ref[pl.ds(x * strip, strip), :] = weights_ref[...] * mask
-        planes = mm(spread_ref[...], plane_ref[...], NT).astype(jnp.bfloat16)
-        rows = pl.ds(pl.multiple_of(step * (group * strip), group * strip), group * strip)
-        field_ref[0, rows, :] = mm(planes, table_ref[0])
-        field_ref[1, rows, :] = mm(planes, table_ref[1])
-        return carry
-
     for step in range(NFFT // group):
-        some_planes(step, 0)
+        for x in range(step * group, (step + 1) * group):
+            spread_ref[pl.ds(x * strip, strip), :] = weights_ref[...] * masks_ref[pl.ds(x, 1), :]
+        some = pl.ds(step * group * strip, group * strip)
+        planes_ref[some, :] = mm(spread_ref[some, :], plane_ref[...], NT).astype(jnp.bfloat16)
+        for u in range(step * group, (step + 1) * group):
+            c, s = cos_line[u : u + 1, :], sin_line[u : u + 1, :]
+            rows = pl.ds(u * PLANE, PLANE)
+            waves_ref[rows, pl.ds(0, strip)] = (cos_plane * c - sin_plane * s).astype(jnp.bfloat16)
+            waves_ref[rows, pl.ds(strip, strip)] = (-(sin_plane * c + cos_plane * s)).astype(jnp.bfloat16)
+    copies[3].wait()
+    fill_orbitals(coefs_ref, table_ref, plane_ref, masks_ref, psi_ref, small_ref, small_field_ref)
+    field_ref[0] = mm(planes_ref[...], table_ref[0])
+    field_ref[1] = mm(planes_ref[...], table_ref[1])
 
     def some_rows(step, carry):
         first = pl.multiple_of(step * 16, 16)
@@ -135,22 +155,12 @@
 
     lax.fori_loop(0, strip // 16, some_rows, 0)
 
-    chosen = plane_ref[:, pl.ds(pl.multiple_of(place_ref[0] * strip, strip), strip)]
-    cos_plane = mm(table_ref[0], chosen)
-    sin_plane = mm(table_ref[1], chosen)
-    level = own_ref[...] >> 8
-    turn = (level * lax.broadcasted_iota(jnp.int32, (NFFT, strip), 0)) & (NFFT - 1)
-    angle = turn.astype(jnp.float32) * (2.0 * math.pi / NFFT)
-    cos_line = jnp.cos(angle)
-    sin_line = jnp.sin(angle)
-    for u in range(NFFT):
-        c, s = cos_line[u : u + 1, :], sin_line[u : u + 1, :]
-        rows = pl.ds(u * PLANE, PLANE)
-        waves_ref[rows, pl.ds(0, strip)] = (cos_plane * c - sin_plane * s).astype(jnp.bfloat16)
-        waves_ref[rows, pl.ds(strip, strip)] = (-(sin_plane * c + cos_plane * s)).astype(jnp.bfloat16)
-
-
-def contract_kernel(scale, here_ref, there_ref, wide_ref, waves_ref, out_ref, valence_ref, conduction_ref):
+
+def contract_kernel(scale, coefs_ref, table_hbm, here_ref, wide_ref, waves_ref, plane_ref, masks_ref, out_ref,
+                    small_ref, small_field_ref, there_ref, valence_ref, conduction_ref, table_ref, sem):
+    copy = pltpu.make_async_copy(table_hbm, table_ref, sem)
+    copy.start()
+    fill_orbitals(coefs_ref, table_ref, plane_ref, masks_ref, there_ref, small_ref, small_field_ref, copy)
     strip = wide_ref.shape[0] // 2
     chunk = 512
     for lane in range(0, GRID, chunk):
@@ -185,71 +195,66 @@
     return lax.ppermute(value, axis, [(i, (i + by) % size) for i in range(size)])
 
 
-def called(kernel, shapes, scratch, flops, moved, *args, smem=0):
-    specs = [pl.BlockSpec(memory_space=pltpu.SMEM)] * smem
-    specs += [pl.BlockSpec(memory_space=pltpu.VMEM)] * (len(args) - smem)
-    out_specs = [pl.BlockSpec(memory_space=pltpu.VMEM) for _ in shapes]
+def called(kernel, shapes, scratch, flops, moved, places, *args):
+    spaces = {"s": pltpu.SMEM, "h": pltpu.HBM, "v": pltpu.VMEM}
+    args = [pltpu.with_memory_space_constraint(a, pltpu.HBM) if p == "h" else a for a, p in zip(args, places)]
     return pl.pallas_call(
         kernel,
         out_shape=shapes,
-        in_specs=specs,
-        out_specs=out_specs,
+        in_specs=[pl.BlockSpec(memory_space=spaces[place]) for place in places],
+        out_specs=[pl.BlockSpec(memory_space=pltpu.VMEM) for _ in shapes],
         scratch_shapes=scratch,
         cost_estimate=pl.CostEstimate(flops=flops, bytes_accessed=moved, transcendentals=0),
         compiler_params=pltpu.CompilerParams(vmem_limit_bytes=36 * 1024 * 1024),
     )(*args)
 
 
-def orbitals(index, coefs, table):
-    bands = coefs.shape[1]
-    shape = jax.ShapeDtypeStruct((2, bands, GRID), jnp.float32)
-    scratch = [
-        pltpu.VMEM((PLANE, NG), jnp.bfloat16),
-        pltpu.VMEM((NFFT, NG), jnp.bfloat16),
-        pltpu.VMEM((2 * NFFT * bands, NG), jnp.bfloat16),
-        pltpu.VMEM((2, 2 * NFFT * bands, PLANE), jnp.float32),
-    ]
-    return called(orbital_kernel, [shape], scratch, 10**9, 2**20, index, coefs, table)[0]
-
-
-def screening_waves(place, index, own, weights, table):
+def small_scratch():
+    rows = 4 * NBND * NFFT
+    return [pltpu.VMEM((rows, NG), jnp.bfloat16), pltpu.VMEM((2, rows, PLANE), jnp.float32)]
+
+
+def prepared(place, index, coefs, weights, table):
     strip = weights.shape[0]
     shapes = [
+        jax.ShapeDtypeStruct((2, 2 * NBND, GRID), jnp.float32),
         jax.ShapeDtypeStruct((2 * strip, GRID), jnp.bfloat16),
         jax.ShapeDtypeStruct((GRID, 2 * strip), jnp.bfloat16),
+        jax.ShapeDtypeStruct((PLANE, NG), jnp.bfloat16),
+        jax.ShapeDtypeStruct((NFFT, NG), jnp.bfloat16),
     ]
-    scratch = [
-        pltpu.VMEM((PLANE, NG), jnp.bfloat16),
-        pltpu.VMEM((NFFT, NG), jnp.bfloat16),
-        pltpu.VMEM((4 * strip, NG), jnp.bfloat16),
+    scratch = small_scratch() + [
+        pltpu.VMEM((NFFT * strip, NG), jnp.bfloat16),
+        pltpu.VMEM((NFFT * strip, PLANE), jnp.bfloat16),
         pltpu.VMEM((2, NFFT * strip, PLANE), jnp.float32),
     ]
-    return called(screen_kernel, shapes, scratch, 5 * 10**9, 2**23, place, index, own, weights, table, smem=1)
-
-
-def contracted(here, there, wide, waves, scale):
+    scratch += [pltpu.VMEM(value.shape, value.dtype) for value in (index, coefs, weights, table)]
+    scratch += [pltpu.SemaphoreType.DMA((4,))]
+    return called(prepare_kernel, shapes, scratch, 6 * 10**9, 2**23, "shhhh", place, index, coefs, weights, table)
+
+
+def contracted(coefs, table, here, wide, waves, plane, masks, scale):
     shape = jax.ShapeDtypeStruct((PAIRS, 2 * PAIRS), jnp.float32)
-    scratch = [pltpu.VMEM((2 * PAIRS, GRID), jnp.bfloat16) for _ in range(2)]
+    scratch = small_scratch() + [pltpu.VMEM((2, 2 * NBND, GRID), jnp.float32)]
+    scratch += [pltpu.VMEM((2 * PAIRS, GRID), jnp.bfloat16) for _ in range(2)]
+    scratch += [pltpu.VMEM(table.shape, table.dtype), pltpu.SemaphoreType.DMA]
 
     def kernel(*refs):
         contract_kernel(scale, *refs)
 
-    return called(kernel, [shape], scratch, 10**9, 2**22, here, there, wide, waves)[0]
+    return called(kernel, [shape], scratch, 10**9, 2**22, "vhvvvvv", coefs, table, here, wide, waves, plane, masks)[0]
 
 
 def body(band_coefs, screening, grid_index):
     width = lax.axis_size("ga")
     place = lax.axis_index("ga").astype(jnp.int32)
-    strip = screening.shape[1]
+    coefs = band_coefs[0]
+    moved = passed_along(coefs, "ka", 1)
     table = jnp.asarray(plane_table(), jnp.bfloat16)
     index = grid_index.reshape(1, NG)
-    coefs = jnp.transpose(band_coefs[0], (1, 0, 2))
-    here = orbitals(index, coefs, table)
-    there = passed_along(here, "ka", 1)
-    own = lax.dynamic_slice_in_dim(index, place * strip, strip, 1)
-    wide, waves = screening_waves(place.reshape(1), index, own, screening[0], table)
+    here, wide, waves, plane, masks = prepared(place.reshape(1), index, coefs, screening[0], table)
     scale = 1.0 / (math.sqrt(NG) * (math.sqrt(GRID) * LEVEL) ** 6)
-    terms = contracted(here, there, wide, waves, scale)
+    terms = contracted(moved, table, here, wide, waves, plane, masks, scale)
     rows = terms.shape[0] // width
     pieces = lax.all_to_all(terms.reshape(width, rows, 2 * PAIRS), "ga", 0, 0, tiled=True)
     return jnp.sum(pieces, axis=0)[None, None]

time: 52.7 us -> 51.1 us (0.970)
  the two profiles are of different devices: /device:TPU:2 before, /device:TPU:49 now
where the time goes in v2:
time: 51.1 us; the launch traced here: 50.9 us
  blocking collectives  32.6 us (64%)
  Pallas kernels  12.5 us (24%)
  starting transfers between devices  5.08 us (10%)
  other arithmetic  0.6 us (1%)
    all_to_all x1, blocking collectives, body(): lax.all_to_all(terms.reshape(width, rows, 2 * PAIRS), 'ga', 0, 0, tiled=T...  32.6 us
    pallas_call x2, Pallas kernels, called(): pl.pallas_call(kernel, out_shape=shapes, in_specs=[pl.BlockSpec(memory_sp...  12.5 us
    ppermute x1, starting transfers between devices, passed_along(): lax.ppermute(value, axis, [(i, (i + by) % size) for i in range(size)])  5.08 us
  transfers between devices with their start and end apart: 1, of which 0 were waited for; matrix products, arithmetic and copies ran while one was open for 0% of the time, Pallas kernels for 16%

profile of v2, /device:TPU:49, one launch (start us, length us, event | category | flops | bytes accessed | tf_op | source)
XLA Modules:
  0.0 50.9 jit_solution(14059131292692896998)
XLA Ops:
  0.0 5.1 %collective-permute-start = (bf16[16,2,2048]{2,1,0:T(2,128)(2,1)}, bf16[16,2,2048]{2,1,0:T(2,128)(2,1)S(1)}, u32[]{:S(2)}, u32[]{:S(2)}) collective-permute-start(bf16[16,2,2048]{2,1,0:T(2,128)(2,1)} %bitcast.8), channel_id=1, source_target_pairs={{0,16},{16,32},{32,48},{48,64},{64,80},{80,96},{96,112},{112,128},... | collective-permute-start | bytes 393224 | tf_op jit(solution)/shard_map/ppermute | solution.py:195
  5.1 8.3 %shard_map.46 = (f32[2,16,4096]{2,1,0:T(8,128)S(1)}, bf16[256,4096]{1,0:T(8,128)(2,1)S(1)}, bf16[4096,256]{1,0:T(8,128)(2,1)S(1)}, bf16[256,2048]{1,0:T(8,128)(2,1)S(1)}, bf16[16,2048]{1,0:T(8,128)(2,1)S(1)}) custom-call(s32[1]{0:T(128)} %bitcast.1.place_ref, s32[1,2048]{1,0:T(1,128)} %bitcast.10, bf16[16,2,2048]{2,1,0:T(2,128)(2,1)} %bitcast.9, ...), custom_call_target="tpu_custom_call" | custom-call | flops 6000000000 | bytes 8388608 | tf_op jit(solution)/shard_map/pallas_call | solution.py:201
  13.4 0.0 collective-permute-done.refs_0_
  13.4 4.2 %shard_map.47 = f32[64,128]{1,0:T(8,128)S(1)} custom-call(bf16[16,2,2048]{2,1,0:T(2,128)(2,1)S(1)} %collective-permute-done.refs_0_, bf16[2,256,256]{2,1,0:T(8,128)(2,1)} %constant.8.clone.table_hbm.refs_1_, f32[2,16,4096]{2,1,0:T(8,128)S(1)} %get-tuple-element.10.refs_2_, bf16[256,4096]{1,0:T(8,128)(2,1)S(1)} %get-tuple-element.11.refs_3_, ...), custom_call_target="tpu_custom_call" | custom-call | flops 1000000000 | bytes 4194304 | tf_op jit(solution)/shard_map/pallas_call | solution.py:201
  17.6 32.6 %all_to_all.5 = f32[16,4,128]{2,1,0:T(4,128)S(1)} all-to-all(f32[16,4,128]{2,1,0:T(4,128)S(1)} %bitcast.6), channel_id=1, replica_groups=mesh['ka'=64,'ga'=16] {'ga'}, dimensions={0} | all-to-all | bytes 65536 | tf_op jit(solution)/shard_map/all_to_all | solution.py:259
  50.2 0.6 %reduce_sum.9 = f32[4,128]{1,0:T(4,128)} reduce(f32[16,4,128]{2,1,0:T(4,128)S(1)} %all_to_all.5, f32[]{:T(128)} %constant.2.clone.1), dimensions={0}, to_apply=%region_0.0 | reduce | flops 7680 | bytes 34820 | tf_op jit(solution)/shard_map/reduce_sum | solution.py:260
Async XLA Ops:
  0.0 13.4 %collective-permute-start = (bf16[16,2,2048]{2,1,0:T(2,128)(2,1)}, bf16[16,2,2048]{2,1,0:T(2,128)(2,1)S(1)}, u32[]{:S(2)}, u32[]{:S(2)}) collective-permute-start(bf16[16,2,2048]{2,1,0:T(2,128)(2,1)} %bitcast.8), channel_id=1, source_target_pairs={{0,16},{16,32},{32,48},{48,64},{64,80},{80,96},{96,112},{112,128},... | collective-permute-start | bytes 393224 | tf_op jit(solution)/shard_map/ppermute | solution.py:195

commit v3 on v2

--- a/solution.py
+++ b/solution.py
@@ -29,7 +29,9 @@
     index = np.arange(PLANE)
     phase = np.outer(index // NFFT, index // NFFT) + np.outer(index % NFFT, index % NFFT)
     angle = (phase % NFFT) * (2.0 * math.pi / NFFT)
-    return np.stack([np.cos(angle), np.sin(angle)]) * STEP
+    cos, sin = np.cos(angle) * STEP, np.sin(angle) * STEP
+    blocks = [np.concatenate([cos[:, at : at + 128], sin[:, at : at + 128]], 1) for at in range(0, PLANE, 128)]
+    return np.stack(blocks + [cos, sin])
 
 
 def radix4(a, b, c, d, sign):
@@ -76,35 +78,42 @@
     masks_ref[...] = jnp.where(levels == (index >> 8), 1.0, 0.0).astype(jnp.bfloat16)
 
 
-def fill_orbitals(coefs_ref, table_ref, plane_ref, masks_ref, psi_ref, spread_ref, field_ref, copy=None):
+def finish_orbitals(block, field_ref, pitch, base, psi_ref):
     bands = 2 * NBND
-    half = NFFT * bands
+    values = []
+    for x in range(NFFT):
+        top, low = pl.ds(x * pitch + base, bands), pl.ds(x * pitch + base + bands, bands)
+        re = field_ref[block, top, pl.ds(0, 128)] - field_ref[block, low, pl.ds(128, 128)]
+        im = field_ref[block, top, pl.ds(128, 128)] + field_ref[block, low, pl.ds(0, 128)]
+        values.append((re, im))
+    for u, (re, im) in enumerate(sixteen(values, 1)):
+        at = pl.ds(u * PLANE + block * 128, 128)
+        psi_ref[0, :, at] = re
+        psi_ref[1, :, at] = im
+
+
+def spread_orbitals(parts_ref, masks_ref, spread_ref, x, pitch, base):
+    bands = 2 * NBND
     for part in range(2):
-        held = coefs_ref[:, part, :]
-        for x in range(NFFT):
-            spread_ref[pl.ds(part * half + x * bands, bands), :] = held * masks_ref[pl.ds(x, 1), :]
+        rows = pl.ds(x * pitch + base + part * bands, bands)
+        spread_ref[rows, :] = parts_ref[part] * masks_ref[pl.ds(x, 1), :]
+
+
+def fill_orbitals(coefs_ref, table_ref, plane_ref, masks_ref, psi_ref, spread_ref, field_ref, parts_ref):
+    for part in range(2):
+        parts_ref[part] = coefs_ref[:, part, :]
+    for x in range(NFFT):
+        spread_orbitals(parts_ref, masks_ref, spread_ref, x, 4 * NBND, 0)
     planes = mm(spread_ref[...], plane_ref[...], NT).astype(jnp.bfloat16)
-    if copy is not None:
-        copy.wait()
-    field_ref[0] = mm(planes, table_ref[0])
-    field_ref[1] = mm(planes, table_ref[1])
-    for lane in range(0, PLANE, 128):
-        at = pl.ds(lane, 128)
-        values = []
-        for x in range(NFFT):
-            top, low = pl.ds(x * bands, bands), pl.ds(half + x * bands, bands)
-            re = field_ref[0, top, at] - field_ref[1, low, at]
-            im = field_ref[1, top, at] + field_ref[0, low, at]
-            values.append((re, im))
-        for u, (re, im) in enumerate(sixteen(values, 1)):
-            psi_ref[0, :, pl.ds(u * PLANE + lane, 128)] = re
-            psi_ref[1, :, pl.ds(u * PLANE + lane, 128)] = im
+    for block in range(2):
+        field_ref[block] = mm(planes, table_ref[block])
+        finish_orbitals(block, field_ref, 4 * NBND, 0, psi_ref)
 
 
 def prepare_kernel(place_ref, index_hbm, coefs_hbm, weights_hbm, table_hbm,
-                   psi_ref, wide_ref, waves_ref, plane_ref, masks_ref,
-                   small_ref, small_field_ref, spread_ref, planes_ref, field_ref,
-                   index_ref, coefs_ref, weights_ref, table_ref, sems):
+                   psi_ref, wide_ref, waves_ref, plane_ref, masks_ref, table_ref,
+                   spread_ref, planes_ref, field_ref,
+                   parts_ref, index_ref, coefs_ref, weights_ref, sems):
     pairs = ((index_hbm, index_ref), (weights_hbm, weights_ref), (table_hbm, table_ref), (coefs_hbm, coefs_ref))
     copies = [pltpu.make_async_copy(source, target, sems.at[i]) for i, (source, target) in enumerate(pairs)]
     for copy in copies:
@@ -120,47 +129,42 @@
     sin_line = jnp.sin(angle)
     copies[1].wait()
     copies[2].wait()
+    copies[3].wait()
+    for part in range(2):
+        parts_ref[part] = coefs_ref[:, part, :]
     chosen = plane_ref[:, pl.ds(first_own, strip)]
-    cos_plane = mm(table_ref[0], chosen)
-    sin_plane = mm(table_ref[1], chosen)
+    cos_plane = mm(table_ref[2], chosen)
+    sin_plane = mm(table_ref[3], chosen)
     group = 4
+    pitch = strip + 4 * NBND
     for step in range(NFFT // group):
         for x in range(step * group, (step + 1) * group):
-            spread_ref[pl.ds(x * strip, strip), :] = weights_ref[...] * masks_ref[pl.ds(x, 1), :]
-        some = pl.ds(step * group * strip, group * strip)
+            spread_ref[pl.ds(x * pitch, strip), :] = weights_ref[...] * masks_ref[pl.ds(x, 1), :]
+            spread_orbitals(parts_ref, masks_ref, spread_ref, x, pitch, strip)
+        some = pl.ds(step * group * pitch, group * pitch)
         planes_ref[some, :] = mm(spread_ref[some, :], plane_ref[...], NT).astype(jnp.bfloat16)
         for u in range(step * group, (step + 1) * group):
             c, s = cos_line[u : u + 1, :], sin_line[u : u + 1, :]
             rows = pl.ds(u * PLANE, PLANE)
             waves_ref[rows, pl.ds(0, strip)] = (cos_plane * c - sin_plane * s).astype(jnp.bfloat16)
             waves_ref[rows, pl.ds(strip, strip)] = (-(sin_plane * c + cos_plane * s)).astype(jnp.bfloat16)
-    copies[3].wait()
-    fill_orbitals(coefs_ref, table_ref, plane_ref, masks_ref, psi_ref, small_ref, small_field_ref)
-    field_ref[0] = mm(planes_ref[...], table_ref[0])
-    field_ref[1] = mm(planes_ref[...], table_ref[1])
-
-    def some_rows(step, carry):
-        first = pl.multiple_of(step * 16, 16)
-        for lane in range(0, PLANE, 128):
-            at = pl.ds(lane, 128)
+    for block in range(2):
+        field_ref[block] = mm(planes_ref[...], table_ref[block])
+        finish_orbitals(block, field_ref, pitch, strip, psi_ref)
+        for first in range(0, strip, 16):
             values = []
             for x in range(NFFT):
-                rows = pl.ds(pl.multiple_of(x * strip + first, 16), 16)
-                values.append((field_ref[0, rows, at], -field_ref[1, rows, at]))
+                rows = pl.ds(x * pitch + first, 16)
+                values.append((field_ref[block, rows, pl.ds(0, 128)], -field_ref[block, rows, pl.ds(128, 128)]))
             for u, (re, im) in enumerate(sixteen(values, -1)):
-                out = pl.ds(u * PLANE + lane, 128)
+                out = pl.ds(u * PLANE + block * 128, 128)
                 wide_ref[pl.ds(first, 16), out] = re.astype(jnp.bfloat16)
-                wide_ref[pl.ds(pl.multiple_of(first + strip, 16), 16), out] = im.astype(jnp.bfloat16)
-        return carry
-
-    lax.fori_loop(0, strip // 16, some_rows, 0)
-
-
-def contract_kernel(scale, coefs_ref, table_hbm, here_ref, wide_ref, waves_ref, plane_ref, masks_ref, out_ref,
-                    small_ref, small_field_ref, there_ref, valence_ref, conduction_ref, table_ref, sem):
-    copy = pltpu.make_async_copy(table_hbm, table_ref, sem)
-    copy.start()
-    fill_orbitals(coefs_ref, table_ref, plane_ref, masks_ref, there_ref, small_ref, small_field_ref, copy)
+                wide_ref[pl.ds(first + strip, 16), out] = im.astype(jnp.bfloat16)
+
+
+def contract_kernel(scale, coefs_ref, here_ref, wide_ref, waves_ref, plane_ref, masks_ref, table_ref, out_ref,
+                    small_ref, small_field_ref, there_ref, valence_ref, conduction_ref, parts_ref):
+    fill_orbitals(coefs_ref, table_ref, plane_ref, masks_ref, there_ref, small_ref, small_field_ref, parts_ref)
     strip = wide_ref.shape[0] // 2
     chunk = 512
     for lane in range(0, GRID, chunk):
@@ -205,7 +209,7 @@
         out_specs=[pl.BlockSpec(memory_space=pltpu.VMEM) for _ in shapes],
         scratch_shapes=scratch,
         cost_estimate=pl.CostEstimate(flops=flops, bytes_accessed=moved, transcendentals=0),
-        compiler_params=pltpu.CompilerParams(vmem_limit_bytes=36 * 1024 * 1024),
+        compiler_params=pltpu.CompilerParams(vmem_limit_bytes=26 * 1024 * 1024),
     )(*args)
 
 
@@ -222,27 +226,30 @@
         jax.ShapeDtypeStruct((GRID, 2 * strip), jnp.bfloat16),
         jax.ShapeDtypeStruct((PLANE, NG), jnp.bfloat16),
         jax.ShapeDtypeStruct((NFFT, NG), jnp.bfloat16),
+        jax.ShapeDtypeStruct(table.shape, table.dtype),
     ]
-    scratch = small_scratch() + [
-        pltpu.VMEM((NFFT * strip, NG), jnp.bfloat16),
-        pltpu.VMEM((NFFT * strip, PLANE), jnp.bfloat16),
-        pltpu.VMEM((2, NFFT * strip, PLANE), jnp.float32),
+    rows = NFFT * (strip + 4 * NBND)
+    scratch = [
+        pltpu.VMEM((rows, NG), jnp.bfloat16),
+        pltpu.VMEM((rows, PLANE), jnp.bfloat16),
+        pltpu.VMEM((2, rows, PLANE), jnp.float32),
+        pltpu.VMEM((2, 2 * NBND, NG), jnp.bfloat16),
     ]
-    scratch += [pltpu.VMEM(value.shape, value.dtype) for value in (index, coefs, weights, table)]
+    scratch += [pltpu.VMEM(value.shape, value.dtype) for value in (index, coefs, weights)]
     scratch += [pltpu.SemaphoreType.DMA((4,))]
     return called(prepare_kernel, shapes, scratch, 6 * 10**9, 2**23, "shhhh", place, index, coefs, weights, table)
 
 
-def contracted(coefs, table, here, wide, waves, plane, masks, scale):
+def contracted(coefs, made, scale):
     shape = jax.ShapeDtypeStruct((PAIRS, 2 * PAIRS), jnp.float32)
     scratch = small_scratch() + [pltpu.VMEM((2, 2 * NBND, GRID), jnp.float32)]
     scratch += [pltpu.VMEM((2 * PAIRS, GRID), jnp.bfloat16) for _ in range(2)]
-    scratch += [pltpu.VMEM(table.shape, table.dtype), pltpu.SemaphoreType.DMA]
+    scratch += [pltpu.VMEM((2, 2 * NBND, NG), jnp.bfloat16)]
 
     def kernel(*refs):
         contract_kernel(scale, *refs)
 
-    return called(kernel, [shape], scratch, 10**9, 2**22, "vhvvvvv", coefs, table, here, wide, waves, plane, masks)[0]
+    return called(kernel, [shape], scratch, 10**9, 2**22, "v" * 7, coefs, *made)[0]
 
 
 def body(band_coefs, screening, grid_index):
@@ -252,9 +259,9 @@
     moved = passed_along(coefs, "ka", 1)
     table = jnp.asarray(plane_table(), jnp.bfloat16)
     index = grid_index.reshape(1, NG)
-    here, wide, waves, plane, masks = prepared(place.reshape(1), index, coefs, screening[0], table)
+    made = prepared(place.reshape(1), index, coefs, screening[0], table)
     scale = 1.0 / (math.sqrt(NG) * (math.sqrt(GRID) * LEVEL) ** 6)
-    terms = contracted(moved, table, here, wide, waves, plane, masks, scale)
+    terms = contracted(moved, made, scale)
     rows = terms.shape[0] // width
     pieces = lax.all_to_all(terms.reshape(width, rows, 2 * PAIRS), "ga", 0, 0, tiled=True)
     return jnp.sum(pieces, axis=0)[None, None]

time: 51.1 us -> 48.3 us (0.945)
  Pallas kernels: 12.5 us -> 9.81 us
    pallas_call x2, Pallas kernels: 12.5 us -> 9.81 us  [called(): pl.pallas_call(kernel, out_shape=shapes, in_specs=[pl.BlockSpec(memory_sp...]
  transfers between devices with their start and end apart: 1 -> 1, of which waited for: 0 -> 0; matrix products, arithmetic and copies ran while one was open for 0% -> 0% of each run, Pallas kernels for 16% -> 14%
where the time goes in v3:
time: 48.3 us; the launch traced here: 48.1 us
  blocking collectives  32.6 us (67%)
  Pallas kernels  9.81 us (20%)
  starting transfers between devices  5.08 us (11%)
  other arithmetic  0.6 us (1%)
    all_to_all x1, blocking collectives, body(): lax.all_to_all(terms.reshape(width, rows, 2 * PAIRS), 'ga', 0, 0, tiled=T...  32.6 us
    pallas_call x2, Pallas kernels, called(): pl.pallas_call(kernel, out_shape=shapes, in_specs=[pl.BlockSpec(memory_sp...  9.81 us
    ppermute x1, starting transfers between devices, passed_along(): lax.ppermute(value, axis, [(i, (i + by) % size) for i in range(size)])  5.08 us
  transfers between devices with their start and end apart: 1, of which 0 were waited for; matrix products, arithmetic and copies ran while one was open for 0% of the time, Pallas kernels for 14%

profile of v3, /device:TPU:49, one launch (start us, length us, event | category | flops | bytes accessed | tf_op | source)
XLA Modules:
  0.0 48.1 jit_solution(11809419854963045118)
XLA Ops:
  0.0 5.1 %collective-permute-start = (bf16[16,2,2048]{2,1,0:T(2,128)(2,1)}, bf16[16,2,2048]{2,1,0:T(2,128)(2,1)S(1)}, u32[]{:S(2)}, u32[]{:S(2)}) collective-permute-start(bf16[16,2,2048]{2,1,0:T(2,128)(2,1)} %bitcast.8), channel_id=1, source_target_pairs={{0,16},{16,32},{32,48},{48,64},{64,80},{80,96},{96,112},{112,128},... | collective-permute-start | bytes 393224 | tf_op jit(solution)/shard_map/ppermute | solution.py:199
  5.1 6.6 %shard_map.46 = (f32[2,16,4096]{2,1,0:T(8,128)S(1)}, bf16[256,4096]{1,0:T(8,128)(2,1)S(1)}, bf16[4096,256]{1,0:T(8,128)(2,1)S(1)}, bf16[256,2048]{1,0:T(8,128)(2...) custom-call(s32[1]{0:T(128)} %bitcast.1.place_ref, s32[1,2048]{1,0:T(1,128)} %bitcast.10, ...), custom_call_target="tpu_custom_call" | custom-call | flops 6000000000 | bytes 8388608 | tf_op jit(solution)/shard_map/pallas_call | solution.py:205
  11.6 0.0 collective-permute-done.refs_0_
  11.7 3.3 %shard_map.47 = f32[64,128]{1,0:T(8,128)S(1)} custom-call(bf16[16,2,2048]{2,1,0:T(2,128)(2,1)S(1)} %collective-permute-done.refs_0_, f32[2,16,4096]{2,1,0:T(8,128)S(1)} %get-tuple-element.11.refs_1_, bf16[256,4096]{1,0:T(8,128)(2,1)S(1)} %get-tuple-element.12.refs_2_, bf16[4096,256]{1,0:T(8,128)(2,1)S(1)} %get-tuple-element.13.refs_3_, ...), custom_call_target="tpu_custom_call" | custom-call | flops 1000000000 | bytes 4194304 | tf_op jit(solution)/shard_map/pallas_call | solution.py:205
  14.9 32.6 %all_to_all.5 = f32[16,4,128]{2,1,0:T(4,128)S(1)} all-to-all(f32[16,4,128]{2,1,0:T(4,128)S(1)} %bitcast.6), channel_id=1, replica_groups=mesh['ka'=64,'ga'=16] {'ga'}, dimensions={0} | all-to-all | bytes 65536 | tf_op jit(solution)/shard_map/all_to_all | solution.py:266
  47.5 0.6 %reduce_sum.9 = f32[4,128]{1,0:T(4,128)} reduce(f32[16,4,128]{2,1,0:T(4,128)S(1)} %all_to_all.5, f32[]{:T(128)} %constant.2.clone.1), dimensions={0}, to_apply=%region_0.0 | reduce | flops 7680 | bytes 34820 | tf_op jit(solution)/shard_map/reduce_sum | solution.py:267
Async XLA Ops:
  0.0 11.7 %collective-permute-start = (bf16[16,2,2048]{2,1,0:T(2,128)(2,1)}, bf16[16,2,2048]{2,1,0:T(2,128)(2,1)S(1)}, u32[]{:S(2)}, u32[]{:S(2)}) collective-permute-start(bf16[16,2,2048]{2,1,0:T(2,128)(2,1)} %bitcast.8), channel_id=1, source_target_pairs={{0,16},{16,32},{32,48},{48,64},{64,80},{80,96},{96,112},{112,128},... | collective-permute-start | bytes 393224 | tf_op jit(solution)/shard_map/ppermute | solution.py:199

commit v4 on v3

--- a/solution.py
+++ b/solution.py
@@ -29,7 +29,7 @@
     index = np.arange(PLANE)
     phase = np.outer(index // NFFT, index // NFFT) + np.outer(index % NFFT, index % NFFT)
     angle = (phase % NFFT) * (2.0 * math.pi / NFFT)
-    cos, sin = np.cos(angle) * STEP, np.sin(angle) * STEP
+    cos, sin = np.cos(angle) * STEP, -np.sin(angle) * STEP
     blocks = [np.concatenate([cos[:, at : at + 128], sin[:, at : at + 128]], 1) for at in range(0, PLANE, 128)]
     return np.stack(blocks + [cos, sin])
 
@@ -83,8 +83,8 @@
     values = []
     for x in range(NFFT):
         top, low = pl.ds(x * pitch + base, bands), pl.ds(x * pitch + base + bands, bands)
-        re = field_ref[block, top, pl.ds(0, 128)] - field_ref[block, low, pl.ds(128, 128)]
-        im = field_ref[block, top, pl.ds(128, 128)] + field_ref[block, low, pl.ds(0, 128)]
+        re = field_ref[block, top, pl.ds(0, 128)] + field_ref[block, low, pl.ds(128, 128)]
+        im = field_ref[block, low, pl.ds(0, 128)] - field_ref[block, top, pl.ds(128, 128)]
         values.append((re, im))
     for u, (re, im) in enumerate(sixteen(values, 1)):
         at = pl.ds(u * PLANE + block * 128, 128)
@@ -108,6 +108,16 @@
     for block in range(2):
         field_ref[block] = mm(planes, table_ref[block])
         finish_orbitals(block, field_ref, 4 * NBND, 0, psi_ref)
+
+
+def store_waves(waves_ref, parity, u, re, im):
+    strip = re.shape[1]
+    re, im = re.astype(jnp.bfloat16), im.astype(jnp.bfloat16)
+    near, far = pl.ds(u * PLANE, PLANE), pl.ds((u + 8) % NFFT * PLANE, PLANE)
+    waves_ref[near, pl.ds(0, strip)] = re
+    waves_ref[near, pl.ds(strip, strip)] = im
+    waves_ref[far, pl.ds(0, strip)] = re * parity
+    waves_ref[far, pl.ds(strip, strip)] = im * parity
 
 
 def prepare_kernel(place_ref, index_hbm, coefs_hbm, weights_hbm, table_hbm,
@@ -123,8 +133,9 @@
     strip = weights_ref.shape[0]
     first_own = pl.multiple_of(place_ref[0] * strip, strip)
     level = index_ref[:, pl.ds(first_own, strip)] >> 8
-    turn = (level * lax.broadcasted_iota(jnp.int32, (NFFT, strip), 0)) & (NFFT - 1)
+    turn = (level * lax.broadcasted_iota(jnp.int32, (8, strip), 0)) & (NFFT - 1)
     angle = turn.astype(jnp.float32) * (2.0 * math.pi / NFFT)
+    parity = (1 - 2 * (level & 1)).astype(jnp.float32).astype(jnp.bfloat16)
     cos_line = jnp.cos(angle)
     sin_line = jnp.sin(angle)
     copies[1].wait()
@@ -143,11 +154,15 @@
             spread_orbitals(parts_ref, masks_ref, spread_ref, x, pitch, strip)
         some = pl.ds(step * group * pitch, group * pitch)
         planes_ref[some, :] = mm(spread_ref[some, :], plane_ref[...], NT).astype(jnp.bfloat16)
-        for u in range(step * group, (step + 1) * group):
-            c, s = cos_line[u : u + 1, :], sin_line[u : u + 1, :]
-            rows = pl.ds(u * PLANE, PLANE)
-            waves_ref[rows, pl.ds(0, strip)] = (cos_plane * c - sin_plane * s).astype(jnp.bfloat16)
-            waves_ref[rows, pl.ds(strip, strip)] = (-(sin_plane * c + cos_plane * s)).astype(jnp.bfloat16)
+        if step == 0:
+            store_waves(waves_ref, parity, 0, cos_plane, sin_plane)
+            c, s = cos_line[4:5, :], sin_line[4:5, :]
+            store_waves(waves_ref, parity, 4, cos_plane * c + sin_plane * s, sin_plane * c - cos_plane * s)
+        else:
+            c, s = cos_line[step : step + 1, :], sin_line[step : step + 1, :]
+            cc, ss, sc, cs = cos_plane * c, sin_plane * s, sin_plane * c, cos_plane * s
+            store_waves(waves_ref, parity, step, cc + ss, sc - cs)
+            store_waves(waves_ref, parity, NFFT - step, cc - ss, sc + cs)
     for block in range(2):
         field_ref[block] = mm(planes_ref[...], table_ref[block])
         finish_orbitals(block, field_ref, pitch, strip, psi_ref)
@@ -155,7 +170,7 @@
             values = []
             for x in range(NFFT):
                 rows = pl.ds(x * pitch + first, 16)
-                values.append((field_ref[block, rows, pl.ds(0, 128)], -field_ref[block, rows, pl.ds(128, 128)]))
+                values.append((field_ref[block, rows, pl.ds(0, 128)], field_ref[block, rows, pl.ds(128, 128)]))
             for u, (re, im) in enumerate(sixteen(values, -1)):
                 out = pl.ds(u * PLANE + block * 128, 128)
                 wide_ref[pl.ds(first, 16), out] = re.astype(jnp.bfloat16)

time: 48.3 us -> 48 us (level)
  transfers between devices with their start and end apart: 1 -> 1, of which waited for: 0 -> 0; matrix products, arithmetic and copies ran while one was open for 0% -> 0% of each run, Pallas kernels for 14% -> 13%
where the time goes in v4:
time: 48 us; the launch traced here: 47.8 us
  blocking collectives  32.6 us (68%)
  Pallas kernels  9.47 us (20%)
  starting transfers between devices  5.08 us (11%)
  other arithmetic  0.6 us (1%)
    all_to_all x1, blocking collectives, body(): lax.all_to_all(terms.reshape(width, rows, 2 * PAIRS), 'ga', 0, 0, tiled=T...  32.6 us
    pallas_call x2, Pallas kernels, called(): pl.pallas_call(kernel, out_shape=shapes, in_specs=[pl.BlockSpec(memory_sp...  9.47 us
    ppermute x1, starting transfers between devices, passed_along(): lax.ppermute(value, axis, [(i, (i + by) % size) for i in range(size)])  5.08 us
  transfers between devices with their start and end apart: 1, of which 0 were waited for; matrix products, arithmetic and copies ran while one was open for 0% of the time, Pallas kernels for 13%

profile of v4, /device:TPU:49, one launch (start us, length us, event | category | flops | bytes accessed | tf_op | source)
XLA Modules:
  0.0 47.8 jit_solution(15578607394350862160)
XLA Ops:
  0.0 5.1 %collective-permute-start = (bf16[16,2,2048]{2,1,0:T(2,128)(2,1)}, bf16[16,2,2048]{2,1,0:T(2,128)(2,1)S(1)}, u32[]{:S(2)}, u32[]{:S(2)}) collective-permute-start(bf16[16,2,2048]{2,1,0:T(2,128)(2,1)} %bitcast.8), channel_id=1, source_target_pairs={{0,16},{16,32},{32,48},{48,64},{64,80},{80,96},{96,112},{112,128},... | collective-permute-start | bytes 393224 | tf_op jit(solution)/shard_map/ppermute | solution.py:214
  5.1 6.2 %shard_map.46 = (f32[2,16,4096]{2,1,0:T(8,128)S(1)}, bf16[256,4096]{1,0:T(8,128)(2,1)S(1)}, bf16[4096,256]{1,0:T(8,128)(2,1)S(1)}, bf16[256,2048]{1,0:T(8,128)(2...) custom-call(s32[1]{0:T(128)} %bitcast.1.place_ref, s32[1,2048]{1,0:T(1,128)} %bitcast.10, ...), custom_call_target="tpu_custom_call" | custom-call | flops 6000000000 | bytes 8388608 | tf_op jit(solution)/shard_map/pallas_call | solution.py:220
  11.3 0.0 collective-permute-done.refs_0_
  11.3 3.3 %shard_map.47 = f32[64,128]{1,0:T(8,128)S(1)} custom-call(bf16[16,2,2048]{2,1,0:T(2,128)(2,1)S(1)} %collective-permute-done.refs_0_, f32[2,16,4096]{2,1,0:T(8,128)S(1)} %get-tuple-element.11.refs_1_, bf16[256,4096]{1,0:T(8,128)(2,1)S(1)} %get-tuple-element.12.refs_2_, bf16[4096,256]{1,0:T(8,128)(2,1)S(1)} %get-tuple-element.13.refs_3_, ...), custom_call_target="tpu_custom_call" | custom-call | flops 1000000000 | bytes 4194304 | tf_op jit(solution)/shard_map/pallas_call | solution.py:220
  14.6 32.6 %all_to_all.5 = f32[16,4,128]{2,1,0:T(4,128)S(1)} all-to-all(f32[16,4,128]{2,1,0:T(4,128)S(1)} %bitcast.6), channel_id=1, replica_groups=mesh['ka'=64,'ga'=16] {'ga'}, dimensions={0} | all-to-all | bytes 65536 | tf_op jit(solution)/shard_map/all_to_all | solution.py:281
  47.2 0.6 %reduce_sum.9 = f32[4,128]{1,0:T(4,128)} reduce(f32[16,4,128]{2,1,0:T(4,128)S(1)} %all_to_all.5, f32[]{:T(128)} %constant.2.clone.1), dimensions={0}, to_apply=%region_0.0 | reduce | flops 7680 | bytes 34820 | tf_op jit(solution)/shard_map/reduce_sum | solution.py:282
Async XLA Ops:
  0.0 11.3 %collective-permute-start = (bf16[16,2,2048]{2,1,0:T(2,128)(2,1)}, bf16[16,2,2048]{2,1,0:T(2,128)(2,1)S(1)}, u32[]{:S(2)}, u32[]{:S(2)}) collective-permute-start(bf16[16,2,2048]{2,1,0:T(2,128)(2,1)} %bitcast.8), channel_id=1, source_target_pairs={{0,16},{16,32},{32,48},{48,64},{64,80},{80,96},{96,112},{112,128},... | collective-permute-start | bytes 393224 | tf_op jit(solution)/shard_map/ppermute | solution.py:214

commit v5 on v4

--- a/solution.py
+++ b/solution.py
@@ -80,16 +80,17 @@
 
 def finish_orbitals(block, field_ref, pitch, base, psi_ref):
     bands = 2 * NBND
-    values = []
-    for x in range(NFFT):
-        top, low = pl.ds(x * pitch + base, bands), pl.ds(x * pitch + base + bands, bands)
-        re = field_ref[block, top, pl.ds(0, 128)] + field_ref[block, low, pl.ds(128, 128)]
-        im = field_ref[block, low, pl.ds(0, 128)] - field_ref[block, top, pl.ds(128, 128)]
-        values.append((re, im))
-    for u, (re, im) in enumerate(sixteen(values, 1)):
-        at = pl.ds(u * PLANE + block * 128, 128)
-        psi_ref[0, :, at] = re
-        psi_ref[1, :, at] = im
+    for half in range(0, bands, 8):
+        values = []
+        for x in range(NFFT):
+            top, low = pl.ds(x * pitch + base + half, 8), pl.ds(x * pitch + base + bands + half, 8)
+            re = field_ref[block, top, pl.ds(0, 128)] + field_ref[block, low, pl.ds(128, 128)]
+            im = field_ref[block, low, pl.ds(0, 128)] - field_ref[block, top, pl.ds(128, 128)]
+            values.append((re, im))
+        for u, (re, im) in enumerate(sixteen(values, 1)):
+            at = pl.ds(u * PLANE + block * 128, 128)
+            psi_ref[0, pl.ds(half, 8), at] = re
+            psi_ref[1, pl.ds(half, 8), at] = im
 
 
 def spread_orbitals(parts_ref, masks_ref, spread_ref, x, pitch, base):

time: 48 us -> 48 us (level)
  no operation moved by 1% of the time
where the time goes in v5:
time: 48 us; the launch traced here: 47.8 us
  blocking collectives  32.6 us (68%)
  Pallas kernels  9.47 us (20%)
  starting transfers between devices  5.08 us (11%)
  other arithmetic  0.6 us (1%)
    all_to_all x1, blocking collectives, body(): lax.all_to_all(terms.reshape(width, rows, 2 * PAIRS), 'ga', 0, 0, tiled=T...  32.6 us
    pallas_call x2, Pallas kernels, called(): pl.pallas_call(kernel, out_shape=shapes, in_specs=[pl.BlockSpec(memory_sp...  9.47 us
    ppermute x1, starting transfers between devices, passed_along(): lax.ppermute(value, axis, [(i, (i + by) % size) for i in range(size)])  5.08 us
  transfers between devices with their start and end apart: 1, of which 0 were waited for; matrix products, arithmetic and copies ran while one was open for 0% of the time, Pallas kernels for 13%

profile of v5, /device:TPU:49, one launch (start us, length us, event | category | flops | bytes accessed | tf_op | source)
XLA Modules:
  0.0 47.8 jit_solution(15578607394350862160)
XLA Ops:
  0.0 5.1 %collective-permute-start = (bf16[16,2,2048]{2,1,0:T(2,128)(2,1)}, bf16[16,2,2048]{2,1,0:T(2,128)(2,1)S(1)}, u32[]{:S(2)}, u32[]{:S(2)}) collective-permute-start(bf16[16,2,2048]{2,1,0:T(2,128)(2,1)} %bitcast.8), channel_id=1, source_target_pairs={{0,16},{16,32},{32,48},{48,64},{64,80},{80,96},{96,112},{112,128},... | collective-permute-start | bytes 393224 | tf_op jit(solution)/shard_map/ppermute | solution.py:215
  5.1 6.2 %shard_map.46 = (f32[2,16,4096]{2,1,0:T(8,128)S(1)}, bf16[256,4096]{1,0:T(8,128)(2,1)S(1)}, bf16[4096,256]{1,0:T(8,128)(2,1)S(1)}, bf16[256,2048]{1,0:T(8,128)(2...) custom-call(s32[1]{0:T(128)} %bitcast.1.place_ref, s32[1,2048]{1,0:T(1,128)} %bitcast.10, ...), custom_call_target="tpu_custom_call" | custom-call | flops 6000000000 | bytes 8388608 | tf_op jit(solution)/shard_map/pallas_call | solution.py:221
  11.3 0.0 collective-permute-done.refs_0_
  11.3 3.3 %shard_map.47 = f32[64,128]{1,0:T(8,128)S(1)} custom-call(bf16[16,2,2048]{2,1,0:T(2,128)(2,1)S(1)} %collective-permute-done.refs_0_, f32[2,16,4096]{2,1,0:T(8,128)S(1)} %get-tuple-element.11.refs_1_, bf16[256,4096]{1,0:T(8,128)(2,1)S(1)} %get-tuple-element.12.refs_2_, bf16[4096,256]{1,0:T(8,128)(2,1)S(1)} %get-tuple-element.13.refs_3_, ...), custom_call_target="tpu_custom_call" | custom-call | flops 1000000000 | bytes 4194304 | tf_op jit(solution)/shard_map/pallas_call | solution.py:221
  14.6 32.6 %all_to_all.5 = f32[16,4,128]{2,1,0:T(4,128)S(1)} all-to-all(f32[16,4,128]{2,1,0:T(4,128)S(1)} %bitcast.6), channel_id=1, replica_groups=mesh['ka'=64,'ga'=16] {'ga'}, dimensions={0} | all-to-all | bytes 65536 | tf_op jit(solution)/shard_map/all_to_all | solution.py:282
  47.2 0.6 %reduce_sum.9 = f32[4,128]{1,0:T(4,128)} reduce(f32[16,4,128]{2,1,0:T(4,128)S(1)} %all_to_all.5, f32[]{:T(128)} %constant.2.clone.1), dimensions={0}, to_apply=%region_0.0 | reduce | flops 7680 | bytes 34820 | tf_op jit(solution)/shard_map/reduce_sum | solution.py:283
Async XLA Ops:
  0.0 11.3 %collective-permute-start = (bf16[16,2,2048]{2,1,0:T(2,128)(2,1)}, bf16[16,2,2048]{2,1,0:T(2,128)(2,1)S(1)}, u32[]{:S(2)}, u32[]{:S(2)}) collective-permute-start(bf16[16,2,2048]{2,1,0:T(2,128)(2,1)} %bitcast.8), channel_id=1, source_target_pairs={{0,16},{16,32},{32,48},{48,64},{64,80},{80,96},{96,112},{112,128},... | collective-permute-start | bytes 393224 | tf_op jit(solution)/shard_map/ppermute | solution.py:215
